TPU v7x, 32 devices: a whole 2x2x4 slice. The times are simulated.
32 devices in a mesh: db: 8 (over z, x), pb: 4 (over y, core).
Axes of the slice: x: 2, y: 2, z: 4, core: 2. Of those that a mesh axis runs over, the one named last changes fastest.
Arguments:
- queries: bfloat16 [256, 4096], P('pb'), may hold values from -6 to 6
- database: bfloat16 [8192, 4096], P(('db', 'pb')), may hold values from -6 to 6
- slopes: int32 [5], replicated, may hold values from 1 to 6, as said below
Outputs:
- match_score: float32 [256, 8192], P(None, ('db', 'pb'))
Inputs may be any that keep to these rules, and one draw needn't show every extreme that they name: `slopes`: every slope lies in 1 to 6; one of them is 6 and one is 1.
All inputs are finite; a program needn't handle non-finite values.
Results may differ from a plain program's by a relative error of at most 0.0003.
Values may be sent and summed in bfloat16 or wider, within the bound.
A program may use at most 64 MiB of HBM per device.

v0:
```python
import jax
import jax.numpy as jnp
from jax import lax
from jax.sharding import PartitionSpec as P

SEQ = 20
RADIUS = 5
SLOPES = 5
SMAX = 6
variance_floor = 0.25


def padded_2(value, sides, width):
    for axis, dim in sides:
        count, length = (lax.axis_size(axis), value.shape[dim])
        up = [(i, (i + 1) % count) for i in range(count - 1)]
        down = [(j, i) for i, j in up]
        last = lax.slice_in_dim(value, length - width, length, axis=dim)
        leading = lax.slice_in_dim(value, 0, width, axis=dim)
        before = lax.ppermute(last, axis, up)
        after = lax.ppermute(leading, axis, down)
        value = jnp.concatenate([before, value, after], axis=dim)
    return value


def from_behind(value, axis, steps):
    count = lax.axis_size(axis)
    leading, last = (max(0, -steps), min(count, count - steps))
    return lax.ppermute(value, axis, [(source, source + steps) for source in range(leading, last)])


def band_mask(first_frame, frame_count, band_total):
    frame_ids = first_frame + jnp.arange(frame_count, dtype=jnp.int32)
    inside = jnp.logical_and(frame_ids >= 0, frame_ids < band_total)
    return inside.astype(jnp.float32)[None, :]


def contrast(extended, validity):
    out_width = extended.shape[1] - 2 * RADIUS
    masked = extended * validity
    squared = masked * masked
    first_sum = masked[:, :out_width]
    second_sum = squared[:, :out_width]
    counted = validity[:, :out_width]
    for offset in range(1, 2 * RADIUS + 1):
        first_sum = first_sum + masked[:, offset : offset + out_width]
        second_sum = second_sum + squared[:, offset : offset + out_width]
        counted = counted + validity[:, offset : offset + out_width]
    counted = jnp.maximum(counted, 1.0)
    average = first_sum / counted
    spread = second_sum / counted - average * average
    center = extended[:, RADIUS : RADIUS + out_width]
    keeper = validity[:, RADIUS : RADIUS + out_width]
    return keeper * (center - average) / jnp.sqrt(jnp.maximum(spread, variance_floor))


def lagged(field, steps, slope):
    col_pad = steps * SMAX
    padded = jnp.pad(field, ((steps, 0), (col_pad, 0)))
    begin = col_pad - steps * slope
    return lax.dynamic_slice(padded, (jnp.int32(0), begin), field.shape)


def window_sum(field, slope):
    powers = [field]
    stride = 1
    while 2 * stride <= SEQ:
        powers.append(powers[-1] + lagged(powers[-1], stride, slope))
        stride = stride * 2
    summed = None
    filled = 0
    for level in reversed(range(len(powers))):
        if SEQ >> level & 1:
            segment = powers[level] if filled == 0 else lagged(powers[level], filled, slope)
            summed = segment if summed is None else summed + segment
            filled = filled + (1 << level)
    return summed


def best_match(joined, slopes, reach):
    highest = None
    for member in range(SLOPES):
        summed = window_sum(joined, slopes[member])[:, reach:]
        highest = summed if highest is None else jnp.maximum(highest, summed)
    return highest * SEQ ** (-0.5)


def on_device(queries, database, slopes):
    frames = database.shape[0]
    scale = database.shape[1] ** (-0.5)
    reach = SMAX * (SEQ - 1)
    band_total = frames * lax.axis_size(("db", "pb"))
    similarity = (
        lax.dot_general(
            lax.all_gather(queries, "pb", axis=0, tiled=True),
            database,
            (((1,), (1,)), ((), ())),
            preferred_element_type=jnp.float32,
        )
        * scale
    )
    anchor = lax.axis_index(("db", "pb")) * frames
    extended = padded_2(similarity, ((("db", "pb"), 1),), RADIUS)
    normed = contrast(extended, band_mask(anchor - RADIUS, frames + 2 * RADIUS, band_total))
    carried = from_behind(normed[:, frames - reach :], ("db", "pb"), 1)
    joined = jnp.concatenate([carried, normed], axis=1)
    return best_match(joined, slopes, reach)


def solution(mesh):
    placed = (P("pb", None), P(("db", "pb"), None), P())
    return jax.shard_map(
        on_device, mesh=mesh, in_specs=placed, out_specs=P(None, ("db", "pb")), check_vma=False
    )
```

profile of v0, /device:TPU:7, one launch (start us, length us, event | category | flops | bytes accessed | tf_op | source)
XLA Modules:
  0.0 78.5 jit_solution(4593972485175373865)
XLA Ops:
  6.5 0.0 copy-start
  6.5 0.0 all-gather.2.cloned.1.call-start
  6.5 0.7 all-gather.2.cloned.1.call-update
  7.3 0.1 fusion.44
  7.4 24.8 %all-gather.2.cloned.1.call-done = bf16[256,4096]{1,0:T(8,128)(2,1)} async-done(((bf16[64,4096]{1,0:T(8,128)(2,1)}), bf16[256,4096]{1,0:T(8,128)(2,1)}) %all-gather.2.cloned.1.call-update) | async-done | bytes 2097168 | tf_op jit(solution)/shard_map/all_gather | solution.py:95
  32.2 0.0 copy-done
  32.2 2.3 %convolution_multiply_fusion = f32[256,256]{0,1:T(8,128)S(1)} fusion(bf16[256,4096]{1,0:T(8,128)(2,1)} %all-gather.2.cloned.1.call-done, bf16[256,4096]{1,0:T(8,128)(2,1)S(1)} %copy-done), kind=kOutput, calls=%fused_computation | convolution fusion | flops 536936448 | bytes 4456448 | tf_op jit(solution)/shard_map/dot_general | solution.py:94
  34.6 4.2 %collective-permute-start = (f32[256,5]{0,1:T(8,128)S(1)}, f32[256,5]{0,1:T(8,128)S(1)}, u32[]{:S(2)}, u32[]{:S(2)}) collective-permute-start(f32[256,5]{0,1:T(8,128)S(1)} %get-tuple-element.12), channel_id=1, source_target_pairs={{0,1},{1,2},{2,3},{3,4},{4,5},{5,6},{6,7},{7,8},{8,9},{9,10},{10,1... | collective-permute-start | bytes 15368 | tf_op jit(solution)/shard_map/ppermute | solution.py:20
  38.7 1.9 %collective-permute-start.1 = (f32[256,5]{0,1:T(8,128)S(1)}, f32[256,5]{0,1:T(8,128)S(1)}, u32[]{:S(2)}, u32[]{:S(2)}) collective-permute-start(f32[256,5]{0,1:T(8,128)S(1)} %get-tuple-element.13), channel_id=1, source_target_pairs={{1,0},{2,1},{3,2},{4,3},{5,4},{6,5},{7,6},{8,7},{9,8},{10,9},{11,1... | collective-permute-start | bytes 15368 | tf_op jit(solution)/shard_map/ppermute | solution.py:21
  40.7 0.0 collective-permute-done
  40.7 4.8 %collective-permute-done.1 = f32[256,5]{0,1:T(8,128)S(1)} collective-permute-done((f32[256,5]{0,1:T(8,128)S(1)}, f32[256,5]{0,1:T(8,128)S(1)}, u32[]{:S(2)}, u32[]{:S(2)}) %collective-permute-start.1) | collective-permute-done | bytes 5152 | tf_op jit(solution)/shard_map/ppermute | solution.py:21
  45.5 0.1 fusion.42
  45.6 0.0 copy-start.1
  45.6 0.5 fusion.34
  46.2 1.9 %collective-permute-start.2 = (f32[256,114]{0,1:T(8,128)S(1)}, f32[256,114]{0,1:T(8,128)S(1)}, u32[]{:S(2)}, u32[]{:S(2)}) collective-permute-start(f32[256,114]{0,1:T(8,128)S(1)} %slice.220), channel_id=1, source_target_pairs={{0,1},{1,2},{2,3},{3,4},{4,5},{5,6},{6,7},{7,8},{8,9},{9,10},{10,1... | collective-permute-start | bytes 350216 | tf_op jit(solution)/shard_map/ppermute | solution.py:29
  48.1 0.0 copy-done.1
  48.2 0.7 fusion.45
  67.1 0.0 collective-permute-done.2
  67.1 0.7 fusion.14
  67.8 0.2 fusion.4
  68.0 0.2 fusion.9
  68.2 0.3 fusion.2
  68.5 0.2 fusion.7
  68.7 0.2 fusion.8
  68.9 0.3 fusion
  69.2 0.2 fusion.5
  69.4 0.2 fusion.6
  69.6 1.2 %fusion.21 = f32[256,256]{0,1:T(8,128)S(1)} fusion(s32[]{:T(128)S(6)} %add.489, f32[256,370]{0,1:T(8,128)S(1)} %fusion.5, s32[]{:T(128)S(6)} %add.491, f32[256,370]{0,1:T(8,128)S(1)} %fusion.6, s32[]{:T(128)S(6)} %add.493, f32[256,370]{0,1:T(8,128)S(1)} %fusion.7, s32[]{:T(128)S(6)} %add.495, f32[256,370]{0,1:T(8,128)S(1)} %fusion.8, s32[]{:T(128)S(6)} %add.497, ...), kind=kLoop, calls=%fused_computation.49 | loop fusion | flops 983040 | bytes 5423144 | tf_op jit(solution)/shard_map/mul | solution.py:85
  70.8 0.8 %copy.4 = f32[256,256]{1,0:T(8,128)} copy(f32[256,256]{0,1:T(8,128)S(1)} %fusion.21) | data formatting | bytes 524288 | tf_op jit(solution)/shard_map/mul | solution.py:85
  (5 shorter events, 0.1 us)
Async XLA Ops:
  6.5 25.7 %copy-start = (bf16[256,4096]{1,0:T(8,128)(2,1)S(1)}, bf16[256,4096]{1,0:T(8,128)(2,1)}, u32[]{:S(2)}) copy-start(bf16[256,4096]{1,0:T(8,128)(2,1)} %param.4) | copy-start | bytes 6291460
  6.5 25.7 %all-gather.2.cloned.1.call-start = ((), (), s32[]{:S(2)}) async-start(), calls=%async_computation | async-start | bytes 2621440 | tf_op jit(solution)/shard_map/all_gather | solution.py:95
  34.6 6.1 %collective-permute-start = (f32[256,5]{0,1:T(8,128)S(1)}, f32[256,5]{0,1:T(8,128)S(1)}, u32[]{:S(2)}, u32[]{:S(2)}) collective-permute-start(f32[256,5]{0,1:T(8,128)S(1)} %get-tuple-element.12), channel_id=1, source_target_pairs={{0,1},{1,2},{2,3},{3,4},{4,5},{5,6},{6,7},{7,8},{8,9},{9,10},{10,1... | collective-permute-start | bytes 15368 | tf_op jit(solution)/shard_map/ppermute | solution.py:20
  38.7 6.8 %collective-permute-start.1 = (f32[256,5]{0,1:T(8,128)S(1)}, f32[256,5]{0,1:T(8,128)S(1)}, u32[]{:S(2)}, u32[]{:S(2)}) collective-permute-start(f32[256,5]{0,1:T(8,128)S(1)} %get-tuple-element.13), channel_id=1, source_target_pairs={{1,0},{2,1},{3,2},{4,3},{5,4},{6,5},{7,6},{8,7},{9,8},{10,9},{11,1... | collective-permute-start | bytes 15368 | tf_op jit(solution)/shard_map/ppermute | solution.py:21
  45.6 2.5 %copy-start.1 = (s32[5]{0:T(128)S(1)}, s32[5]{0:T(128)}, u32[]{:S(2)}) copy-start(s32[5]{0:T(128)} %param.5) | copy-start | bytes 64
  46.2 20.9 %collective-permute-start.2 = (f32[256,114]{0,1:T(8,128)S(1)}, f32[256,114]{0,1:T(8,128)S(1)}, u32[]{:S(2)}, u32[]{:S(2)}) collective-permute-start(f32[256,114]{0,1:T(8,128)S(1)} %slice.220), channel_id=1, source_target_pairs={{0,1},{1,2},{2,3},{3,4},{4,5},{5,6},{6,7},{7,8},{8,9},{9,10},{10,1... | collective-permute-start | bytes 350216 | tf_op jit(solution)/shard_map/ppermute | solution.py:29
Sparse Core Ops, SparseCore 0:
  8.9 23.2 all-gather.1
where the time goes:
time: 78.9 us; the launch traced here: 78.5 us
  between operations  31.8 us (40%)
  waiting for transfers between devices  30.4 us (39%)
  starting transfers between devices  8.05 us (10%)
  other arithmetic  4.36 us (6%)
  matrix products  2.33 us (3%)
  local copies, waits for them, and re-layouts  1.52 us (2%)
    all_gather x1, waiting for transfers between devices, on_device(): lax.all_gather(queries, 'pb', axis=0, tiled=True)  24.8 us
    ppermute x1, waiting for transfers between devices, padded_2(): after = lax.ppermute(leading, axis, down)  4.81 us
    ppermute x1, starting transfers between devices, padded_2(): before = lax.ppermute(last, axis, up)  4.18 us
    add x9, other arithmetic, window_sum(): powers.append(powers[-1] + lagged(powers[-1], stride, slope))  2.43 us
    dot_general x1, matrix products, on_device(): lax.dot_general(lax.all_gather(queries, 'pb', axis=0, tiled=True), databa...  2.33 us
    ppermute x1, starting transfers between devices, from_behind(): lax.ppermute(value, axis, [(source, source + steps) for source in range(l...  1.94 us
    ppermute x1, starting transfers between devices, padded_2(): after = lax.ppermute(leading, axis, down)  1.92 us
  transfers between devices with their start and end apart: 4, of which 2 were waited for; matrix products, arithmetic and copies ran while one was open for 1% of the time, Pallas kernels for 0%

commit v1 on v0

--- a/solution.py
+++ b/solution.py
@@ -2,12 +2,34 @@
 import jax.numpy as jnp
 from jax import lax
 from jax.sharding import PartitionSpec as P
+from jax.lax import axis_index, ppermute, psum
 
 SEQ = 20
 RADIUS = 5
 SLOPES = 5
 SMAX = 6
 variance_floor = 0.25
+
+
+def handle_ports(payload, row_dim):
+    b_now = list(payload.shape[1:])
+    b_now[row_dim] *= payload.shape[0]
+    return jnp.moveaxis(payload, 0, row_dim).reshape(b_now)
+
+
+def move_the_ranges(in_array, bus_axis):
+    lower, found_now = (psum(1, bus_axis), axis_index(bus_axis))
+    next_value, state_now = (in_array[None], 1)
+    while state_now < lower:
+        current_block = ppermute(
+            next_value, bus_axis, [(dev_j, dev_j ^ state_now) for dev_j in range(lower)]
+        )
+        near = found_now & state_now == 0
+        next_value = jnp.concatenate(
+            [jnp.where(near, next_value, current_block), jnp.where(near, current_block, next_value)]
+        )
+        state_now *= 2
+    return next_value
 
 
 def padded_2(value, sides, width):
@@ -90,9 +112,13 @@
     scale = database.shape[1] ** (-0.5)
     reach = SMAX * (SEQ - 1)
     band_total = frames * lax.axis_size(("db", "pb"))
+
+    def step_on_zone_here(vals, t0, axis_k):
+        return handle_ports(move_the_ranges(vals, t0), axis_k)
+
     similarity = (
         lax.dot_general(
-            lax.all_gather(queries, "pb", axis=0, tiled=True),
+            step_on_zone_here(queries, "pb", axis_k=0),
             database,
             (((1,), (1,)), ((), ())),
             preferred_element_type=jnp.float32,

time: 78.9 us -> 69.6 us (0.88)
  between operations: 31.8 us -> 18.7 us
  other arithmetic: 4.36 us -> 8.22 us
  matrix products: 2.33 us -> 0.74 us
  starting transfers between devices: 8.05 us -> 8.97 us
    ppermute x0 -> x2, waiting for transfers between devices: none -> 26.2 us  [move_the_ranges(): ppermute(next_value, bus_axis, [(dev_j, dev_j ^ state_now) for dev_j in r...]
    all_gather x1 -> x0, waiting for transfers between devices: 24.8 us -> none  [on_device(): lax.all_gather(queries, 'pb', axis=0, tiled=True)]
    select_n x0 -> x2, other arithmetic: none -> 2.63 us  [move_the_ranges(): jnp.where(near, next_value, current_block)]
    dot_general x1, matrix products: 2.33 us -> 0.74 us  [on_device(): lax.dot_general(step_on_zone_here(queries, 'pb', axis_k=0), database, (((...]
    concatenate x0 -> x2, other arithmetic: none -> 1.26 us  [move_the_ranges(): jnp.concatenate([jnp.where(near, next_value, current_block), jnp.where(ne...]
    ppermute x0 -> x2, starting transfers between devices: none -> 0.9 us  [move_the_ranges(): ppermute(next_value, bus_axis, [(dev_j, dev_j ^ state_now) for dev_j in r...]
  transfers between devices with their start and end apart: 4 -> 5, of which waited for: 2 -> 3; matrix products, arithmetic and copies ran while one was open for 1% -> 1% of each run, Pallas kernels for 0% -> 0%
where the time goes in v1:
time: 69.6 us; the launch traced here: 69.2 us
  waiting for transfers between devices  31.1 us (45%)
  between operations  18.7 us (27%)
  starting transfers between devices  8.97 us (13%)
  other arithmetic  8.22 us (12%)
  local copies, waits for them, and re-layouts  1.51 us (2%)
  matrix products  0.74 us (1%)
    ppermute x2, waiting for transfers between devices, move_the_ranges(): ppermute(next_value, bus_axis, [(dev_j, dev_j ^ state_now) for dev_j in r...  26.2 us
    ppermute x1, waiting for transfers between devices, padded_2(): after = lax.ppermute(leading, axis, down)  4.82 us
    ppermute x1, starting transfers between devices, padded_2(): before = lax.ppermute(last, axis, up)  4.2 us
    select_n x2, other arithmetic, move_the_ranges(): jnp.where(near, next_value, current_block)  2.63 us
    add x9, other arithmetic, window_sum(): powers.append(powers[-1] + lagged(powers[-1], stride, slope))  2.41 us
    ppermute x1, starting transfers between devices, from_behind(): lax.ppermute(value, axis, [(source, source + steps) for source in range(l...  1.94 us
    ppermute x1, starting transfers between devices, padded_2(): after = lax.ppermute(leading, axis, down)  1.92 us
  transfers between devices with their start and end apart: 5, of which 3 were waited for; matrix products, arithmetic and copies ran while one was open for 1% of the time, Pallas kernels for 0%

profile of v1, /device:TPU:7, one launch (start us, length us, event | category | flops | bytes accessed | tf_op | source)
XLA Modules:
  0.0 69.2 jit_solution(15185940197901406751)
XLA Ops:
  0.0 0.0 copy-start
  0.0 0.7 collective-permute-start
  0.7 1.9 %collective-permute-done = bf16[1,64,4096]{2,1,0:T(8,128)(2,1)} collective-permute-done((bf16[1,64,4096]{2,1,0:T(8,128)(2,1)}, bf16[1,64,4096]{2,1,0:T(8,128)(2,1)}, u32[]{:S(2)}, u32[]{:S(2)}) %collective-permute-start) | collective-permute-done | bytes 524320 | tf_op jit(solution)/shard_map/ppermute | solution.py:24
  2.6 1.3 %broadcast_select_fusion.3 = (bf16[1,64,4096]{2,1,0:T(8,128)(2,1)S(1)}, bf16[1,64,4096]{2,1,0:T(8,128)(2,1)S(1)}) fusion(bf16[1,64,4096]{2,1,0:T(8,128)(2,1)} %collective-permute-done, pred[]{:T(512)S(6)} %eq.7, bf16[64,4096]{1,0:T(8,128)(2,1)} %param.3), kind=kLoop, calls=%fused_computation.31 | loop fusion | flops 524288 | bytes 2097153 | tf_op jit(solution)/shard_map/jit(_where)/select_n | solution.py:29
  3.8 1.1 %pad_maximum_fusion.1 = bf16[2,64,4096]{2,1,0:T(8,128)(2,1)} fusion(bf16[1,64,4096]{2,1,0:T(8,128)(2,1)S(1)} %get-tuple-element.10, bf16[1,64,4096]{2,1,0:T(8,128)(2,1)S(1)} %get-tuple-element.9), kind=kLoop, calls=%fused_computation.2 | loop fusion | flops 524288 | bytes 2097152 | tf_op jit(solution)/shard_map/concatenate | solution.py:28
  4.9 0.2 collective-permute-start.1
  5.1 0.1 fusion.44
  5.2 24.4 %collective-permute-done.1 = bf16[2,64,4096]{2,1,0:T(8,128)(2,1)} collective-permute-done((bf16[2,64,4096]{2,1,0:T(8,128)(2,1)}, bf16[2,64,4096]{2,1,0:T(8,128)(2,1)}, u32[]{:S(2)}, u32[]{:S(2)}) %collective-permute-start.1) | collective-permute-done | bytes 1048608 | tf_op jit(solution)/shard_map/ppermute | solution.py:24
  29.6 1.4 %broadcast_select_fusion.1 = (bf16[2,64,4096]{2,1,0:T(8,128)(2,1)S(1)}, bf16[2,64,4096]{2,1,0:T(8,128)(2,1)S(1)}) fusion(bf16[2,64,4096]{2,1,0:T(8,128)(2,1)} %collective-permute-done.1, pred[]{:T(512)S(6)} %eq.6, bf16[1,64,4096]{2,1,0:T(8,128)(2,1)S(1)} %get-tuple-element.10, bf16[1,64,4096]{2,1,0:T(8,128)(2,1)S(1)} %get-tuple-element.9), kind=kLoop, calls=%fused_computation.4 | loop fusion | flops 1572864 | bytes 4194305 | tf_op jit(solution)/shard_map/jit(_where)/select_n | solution.py:29
  31.0 0.2 pad_maximum_fusion
  31.2 0.0 copy-done
  31.2 0.7 %convolution_multiply_fusion = f32[256,256]{0,1:T(8,128)S(1)} fusion(bf16[256,4096]{1,0:T(8,128)(2,1)S(1)} %bitcast.58, bf16[256,4096]{1,0:T(8,128)(2,1)S(1)} %copy-done), kind=kOutput, calls=%fused_computation.1 | convolution fusion | flops 536936448 | bytes 4456448 | tf_op jit(solution)/shard_map/dot_general | solution.py:120
  31.9 4.2 %collective-permute-start.2 = (f32[256,5]{0,1:T(8,128)S(1)}, f32[256,5]{0,1:T(8,128)S(1)}, u32[]{:S(2)}, u32[]{:S(2)}) collective-permute-start(f32[256,5]{0,1:T(8,128)S(1)} %get-tuple-element.16), channel_id=1, source_target_pairs={{0,1},{1,2},{2,3},{3,4},{4,5},{5,6},{6,7},{7,8},{8,9},{9,10},{10,1... | collective-permute-start | bytes 15368 | tf_op jit(solution)/shard_map/ppermute | solution.py:42
  36.1 1.9 %collective-permute-start.3 = (f32[256,5]{0,1:T(8,128)S(1)}, f32[256,5]{0,1:T(8,128)S(1)}, u32[]{:S(2)}, u32[]{:S(2)}) collective-permute-start(f32[256,5]{0,1:T(8,128)S(1)} %get-tuple-element.17), channel_id=1, source_target_pairs={{1,0},{2,1},{3,2},{4,3},{5,4},{6,5},{7,6},{8,7},{9,8},{10,9},{11,1... | collective-permute-start | bytes 15368 | tf_op jit(solution)/shard_map/ppermute | solution.py:43
  38.1 0.0 collective-permute-done.2
  38.1 4.8 %collective-permute-done.3 = f32[256,5]{0,1:T(8,128)S(1)} collective-permute-done((f32[256,5]{0,1:T(8,128)S(1)}, f32[256,5]{0,1:T(8,128)S(1)}, u32[]{:S(2)}, u32[]{:S(2)}) %collective-permute-start.3) | collective-permute-done | bytes 5152 | tf_op jit(solution)/shard_map/ppermute | solution.py:43
  42.9 0.1 fusion.42
  43.0 0.0 copy-start.1
  43.0 0.5 fusion.34
  43.6 1.9 %collective-permute-start.4 = (f32[256,114]{0,1:T(8,128)S(1)}, f32[256,114]{0,1:T(8,128)S(1)}, u32[]{:S(2)}, u32[]{:S(2)}) collective-permute-start(f32[256,114]{0,1:T(8,128)S(1)} %slice.220), channel_id=1, source_target_pairs={{0,1},{1,2},{2,3},{3,4},{4,5},{5,6},{6,7},{7,8},{8,9},{9,10},{10,1... | collective-permute-start | bytes 350216 | tf_op jit(solution)/shard_map/ppermute | solution.py:51
  45.5 0.0 copy-done.1
  45.5 0.6 fusion.45
  64.7 0.0 collective-permute-done.4
  64.7 0.6 fusion.14
  65.4 0.3 fusion.2
  65.7 0.2 fusion.8
  65.9 0.2 fusion.7
  66.1 0.3 fusion
  66.4 0.2 fusion.6
  66.6 0.2 fusion.5
  66.8 0.2 fusion.4
  67.0 0.2 fusion.9
  67.2 1.2 %fusion.21 = f32[256,256]{0,1:T(8,128)S(1)} fusion(s32[]{:T(128)S(6)} %add.489, f32[256,370]{0,1:T(8,128)S(1)} %fusion.5, s32[]{:T(128)S(6)} %add.491, f32[256,370]{0,1:T(8,128)S(1)} %fusion.6, s32[]{:T(128)S(6)} %add.493, f32[256,370]{0,1:T(8,128)S(1)} %fusion.7, s32[]{:T(128)S(6)} %add.495, f32[256,370]{0,1:T(8,128)S(1)} %fusion.8, s32[]{:T(128)S(6)} %add.497, ...), kind=kLoop, calls=%fused_computation.55 | loop fusion | flops 983040 | bytes 5423144 | tf_op jit(solution)/shard_map/mul | solution.py:107
  68.3 0.8 %copy.4 = f32[256,256]{1,0:T(8,128)} copy(f32[256,256]{0,1:T(8,128)S(1)} %fusion.21) | data formatting | bytes 524288 | tf_op jit(solution)/shard_map/mul | solution.py:107
  (5 shorter events, 0.1 us)
Async XLA Ops:
  0.0 31.2 %copy-start = (bf16[256,4096]{1,0:T(8,128)(2,1)S(1)}, bf16[256,4096]{1,0:T(8,128)(2,1)}, u32[]{:S(2)}) copy-start(bf16[256,4096]{1,0:T(8,128)(2,1)} %param.4) | copy-start | bytes 6291460
  0.0 2.6 %collective-permute-start = (bf16[1,64,4096]{2,1,0:T(8,128)(2,1)}, bf16[1,64,4096]{2,1,0:T(8,128)(2,1)}, u32[]{:S(2)}, u32[]{:S(2)}) collective-permute-start(bf16[1,64,4096]{2,1,0:T(8,128)(2,1)} %bitcast.59), channel_id=1, source_target_pairs={{0,1},{1,0},{2,3},{3,2},{4,5},{5,4},{6,7},{7,6},{8,9},{9,8},{10,11... | collective-permute-start | bytes 1572872 | tf_op jit(solution)/shard_map/ppermute | solution.py:24
  4.9 24.7 %collective-permute-start.1 = (bf16[2,64,4096]{2,1,0:T(8,128)(2,1)}, bf16[2,64,4096]{2,1,0:T(8,128)(2,1)}, u32[]{:S(2)}, u32[]{:S(2)}) collective-permute-start(bf16[2,64,4096]{2,1,0:T(8,128)(2,1)} %pad_maximum_fusion.1), channel_id=1, source_target_pairs={{0,2},{1,3},{2,0},{3,1},{4,6},{5,7},{6,4},{7,5},{8,10},{9,11},{10,... | collective-permute-start | bytes 3145736 | tf_op jit(solution)/shard_map/ppermute | solution.py:24
  31.9 6.2 %collective-permute-start.2 = (f32[256,5]{0,1:T(8,128)S(1)}, f32[256,5]{0,1:T(8,128)S(1)}, u32[]{:S(2)}, u32[]{:S(2)}) collective-permute-start(f32[256,5]{0,1:T(8,128)S(1)} %get-tuple-element.16), channel_id=1, source_target_pairs={{0,1},{1,2},{2,3},{3,4},{4,5},{5,6},{6,7},{7,8},{8,9},{9,10},{10,1... | collective-permute-start | bytes 15368 | tf_op jit(solution)/shard_map/ppermute | solution.py:42
  36.1 6.8 %collective-permute-start.3 = (f32[256,5]{0,1:T(8,128)S(1)}, f32[256,5]{0,1:T(8,128)S(1)}, u32[]{:S(2)}, u32[]{:S(2)}) collective-permute-start(f32[256,5]{0,1:T(8,128)S(1)} %get-tuple-element.17), channel_id=1, source_target_pairs={{1,0},{2,1},{3,2},{4,3},{5,4},{6,5},{7,6},{8,7},{9,8},{10,9},{11,1... | collective-permute-start | bytes 15368 | tf_op jit(solution)/shard_map/ppermute | solution.py:43
  43.0 2.5 %copy-start.1 = (s32[5]{0:T(128)S(1)}, s32[5]{0:T(128)}, u32[]{:S(2)}) copy-start(s32[5]{0:T(128)} %param.5) | copy-start | bytes 64
  43.6 21.1 %collective-permute-start.4 = (f32[256,114]{0,1:T(8,128)S(1)}, f32[256,114]{0,1:T(8,128)S(1)}, u32[]{:S(2)}, u32[]{:S(2)}) collective-permute-start(f32[256,114]{0,1:T(8,128)S(1)} %slice.220), channel_id=1, source_target_pairs={{0,1},{1,2},{2,3},{3,4},{4,5},{5,6},{6,7},{7,8},{8,9},{9,10},{10,1... | collective-permute-start | bytes 350216 | tf_op jit(solution)/shard_map/ppermute | solution.py:51
